TPU v7x, 512 devices: a whole 4x4x16 slice. The times are simulated.
512 devices in a mesh: tile: 128 (over x, z, core), rep: 4 (over y).
Axes of the slice: x: 4, y: 4, z: 16, core: 2. Of those that a mesh axis runs over, the one named last changes fastest.
Arguments:
- embedding: bfloat16 [2048, 64, 256], P('tile'), may hold values from -6 to 6
- prompt_tile: int32 [65536, 1], P(('tile', 'rep')), may hold values from 0 to 127; in each aligned block of 128 rows (0 to 127, 128 to 255, ...) at most 2 rows name the same one
- crop_row: int32 [65536], P(('tile', 'rep')), may hold values from 0 to 15
- crop_col: int32 [65536], P(('tile', 'rep')), may hold values from 0 to 60
- points: int32 [65536, 2], P(('tile', 'rep')), may hold values from 0 to 15
- confidence: int32 [65536], P(('tile', 'rep')), may hold values from 1 to 4
- pe_matrix: float32 [2, 128], replicated, may hold values from -5 to 5
- point_embed: float32 [256], replicated, may hold values from -5 to 5
- w_one: bfloat16 [256, 256], replicated, may hold values from -0.375 to 0.375
- w_two: bfloat16 [256, 256], replicated, may hold values from -0.375 to 0.375
- w_three: bfloat16 [256, 32], replicated, may hold values from -0.375 to 0.375
- conv_one: bfloat16 [256, 256], replicated, may hold values from -0.375 to 0.375
- conv_two: bfloat16 [64, 128], replicated, may hold values from -0.75 to 0.75
Outputs:
- mask_sum: float32 [8192, 256], P('tile')
Inputs may be any that keep to these rules, and one draw needn't show every extreme that they name: `prompt_tile`: among the prompts of one device no strip is named more than 2 times, and some device names some strip exactly 2 times.
All inputs are finite; a program needn't handle non-finite values.
Results may differ from a plain program's by a relative error of at most 0.0049.
Values may be sent and summed in bfloat16 or wider, within the bound.
No kernel may reach another device: no remote copies, remote signals or barrier semaphores. Data moves between devices by JAX's collectives and lax.ppermute only.
A program may use at most 64 MiB of HBM per device.

v0:
```python
import math
import jax
import jax.numpy as jnp
from jax import lax
from jax.sharding import PartitionSpec as P

CK = 4


def shifted(value, axis, steps):
    count = lax.axis_size(axis)
    leading, last = (max(0, -steps), min(count, count - steps))
    return lax.ppermute(value, axis, [(source, source + steps) for source in range(leading, last)])


def prompt_heads(points, pe_matrix, point_embed, w_one, w_two, w_three):
    coords = (points.astype(jnp.float32) + 0.5) / (4.0 * CK) * 2.0 - 1.0
    angles = (coords[:, 0:1] * pe_matrix[0][None, :] + coords[:, 1:2] * pe_matrix[1][None, :]) * (
        2.0 * math.pi
    )
    tokens = (
        jnp.concatenate([jnp.sin(angles), jnp.cos(angles)], axis=1) + point_embed[None, :]
    ).astype(jnp.bfloat16)
    hidden_one = jax.nn.relu(jnp.dot(tokens, w_one, preferred_element_type=jnp.float32)).astype(
        jnp.bfloat16
    )
    hidden_two = jax.nn.relu(jnp.dot(hidden_one, w_two, preferred_element_type=jnp.float32)).astype(
        jnp.bfloat16
    )
    return jnp.dot(hidden_two, w_three, preferred_element_type=jnp.float32).astype(jnp.bfloat16)


def mask_terms(crop_cells, head_rows, scale_rows, conv_one, conv_two):
    amount, crop_side, channels = (crop_cells.shape[0], crop_cells.shape[1], crop_cells.shape[3])
    mid_width = conv_one.shape[1] // 4
    narrow = conv_two.shape[1] // 4
    first_up = jnp.dot(
        crop_cells.reshape(amount * crop_side * crop_side, channels),
        conv_one,
        preferred_element_type=jnp.float32,
    )
    first_up = first_up.reshape(amount * crop_side * crop_side * 4, mid_width)
    centre = first_up - jnp.mean(first_up, axis=1, keepdims=True)
    normed = centre * lax.rsqrt(jnp.mean(centre * centre, axis=1, keepdims=True) + 1e-06)
    active = jax.nn.gelu(normed, approximate=False).astype(jnp.bfloat16)
    second = jnp.dot(active, conv_two, preferred_element_type=jnp.float32)
    upscaled = (
        jax.nn.gelu(second, approximate=False)
        .astype(jnp.bfloat16)
        .reshape(amount, crop_side * crop_side * 16, narrow)
    )
    logits = jnp.einsum("nqc,nc->nq", upscaled, head_rows, preferred_element_type=jnp.float32)
    logits = logits.reshape(amount, crop_side, crop_side, 2, 2, 2, 2).transpose(0, 1, 3, 5, 2, 4, 6)
    logits = logits.reshape(amount, 4 * crop_side, 4 * crop_side)
    return (logits * scale_rows[:, None, None]).astype(jnp.bfloat16)


def terms_in_blocks(crop_cells, head_rows, scale_rows, conv_one, conv_two):
    amount = crop_cells.shape[0]
    block_size = 64
    groups = amount // block_size

    def one_block(group_in):
        return mask_terms(group_in[0], group_in[1], group_in[2], conv_one, conv_two)

    result = lax.map(
        one_block,
        (
            crop_cells.reshape((groups, block_size) + crop_cells.shape[1:]),
            head_rows.reshape(groups, block_size, head_rows.shape[1]),
            scale_rows.reshape(groups, block_size),
        ),
    )
    return result.reshape((amount,) + result.shape[2:])


def cut_crops(extended, row_starts, col_starts):
    height, width, channels = (extended.shape[0], extended.shape[1], extended.shape[2])
    offsets = jnp.arange(CK, dtype=jnp.int32)
    cell_rows = row_starts.astype(jnp.int32)[:, None, None] + offsets[None, :, None]
    cell_cols = col_starts.astype(jnp.int32)[:, None, None] + offsets[None, None, :]
    cell_index = (cell_rows * width + cell_cols).reshape(-1)
    picked = jnp.take(extended.reshape(height * width, channels), cell_index, axis=0)
    return picked.reshape(row_starts.shape[0], CK, CK, channels)


def place_patches(patches, row_starts, col_starts, height, breadth):
    amount, patch_side = (patches.shape[0], patches.shape[1])
    block_size = 64
    groups = amount // block_size
    offsets = jnp.arange(patch_side, dtype=jnp.int32)
    canvas_rows = jnp.arange(height, dtype=jnp.int32)
    canvas_cols = jnp.arange(breadth, dtype=jnp.int32)

    def add_block(canvas, block_in):
        patch_in, row_at, col_at = block_in
        col_table = (
            4 * col_at[:, None, None] + offsets[None, :, None] == canvas_cols[None, None, :]
        ).astype(jnp.bfloat16)
        placed = jnp.einsum(
            "byx,bxs->bys", patch_in, col_table, preferred_element_type=jnp.float32
        ).astype(jnp.bfloat16)
        row_table = (
            4 * row_at[:, None, None] + offsets[None, :, None] == canvas_rows[None, None, :]
        ).astype(jnp.bfloat16)
        added = jnp.einsum(
            "kr,ks->rs",
            row_table.reshape(block_size * patch_side, height),
            placed.reshape(block_size * patch_side, breadth),
            preferred_element_type=jnp.float32,
        )
        return (canvas + added, None)

    canvas, unused = lax.scan(
        add_block,
        jnp.zeros((height, breadth), jnp.float32),
        (
            patches.reshape(groups, block_size, patch_side, patch_side),
            row_starts.reshape(groups, block_size),
            col_starts.reshape(groups, block_size),
        ),
    )
    return canvas


def on_device(
    embedding,
    prompt_tile,
    crop_row,
    crop_col,
    points,
    confidence,
    pe_matrix,
    point_embed,
    w_one,
    w_two,
    w_three,
    conv_one,
    conv_two,
):
    tile_count = lax.axis_size("tile")
    strip_height = embedding.shape[0]
    breadth = 4 * embedding.shape[1]
    prompt_count = prompt_tile.shape[0]
    slot_most = max(2, 2 * prompt_count // tile_count)
    slot_total = tile_count * slot_most
    dynamic_heads = prompt_heads(points, pe_matrix, point_embed, w_one, w_two, w_three)
    head_width = dynamic_heads.shape[1]
    target = prompt_tile[:, 0]
    onehot = (target[:, None] == jnp.arange(tile_count, dtype=jnp.int32)[None, :]).astype(jnp.int32)
    earlier = jnp.cumsum(onehot, axis=0) - onehot
    rank_in = jnp.sum(earlier * onehot, axis=1)
    slot_index = target * slot_most + rank_in
    request = jnp.stack([crop_row, crop_col, confidence], axis=1)
    request_slots = (
        jnp.zeros((slot_total, 3), jnp.int32)
        .at[slot_index]
        .set(request)
        .reshape(tile_count, slot_most, 3)
    )
    rows_below = shifted(embedding[: CK - 1], "tile", -1)
    extended = jnp.concatenate([embedding, rows_below], axis=0)
    head_slots = jnp.zeros((slot_total, head_width), jnp.bfloat16).at[slot_index].set(dynamic_heads)
    head_slots = head_slots.reshape(tile_count, slot_most, head_width)
    head_in = lax.all_to_all(head_slots, "tile", split_axis=0, concat_axis=0, tiled=True)
    request_in = lax.all_to_all(request_slots, "tile", split_axis=0, concat_axis=0, tiled=True)
    sources = request_in.shape[0]
    per_source = request_in.shape[1]
    flat_request = request_in.reshape(sources * per_source, 3)
    crop_cells = cut_crops(extended, flat_request[:, 0], flat_request[:, 1])
    patches = terms_in_blocks(
        crop_cells,
        head_in.reshape(sources * per_source, head_width),
        flat_request[:, 2].astype(jnp.float32) / 4.0,
        conv_one,
        conv_two,
    )
    patch_slots = patches.reshape(sources, per_source, 4 * CK, 4 * CK)
    owner_flat = request_in.reshape(slot_total, 3)
    canvas = place_patches(
        patch_slots.reshape(slot_total, 4 * CK, 4 * CK),
        owner_flat[:, 0],
        owner_flat[:, 1],
        4 * strip_height + 4 * CK - 4,
        breadth,
    )
    summed = lax.psum(canvas, "rep")
    spilled = shifted(summed[4 * strip_height :], "tile", 1)
    return summed[: 4 * strip_height] + jnp.pad(
        spilled, ((0, 4 * strip_height - spilled.shape[0]), (0, 0))
    )


def solution(mesh):
    return jax.shard_map(
        on_device,
        mesh=mesh,
        in_specs=(
            P("tile", None, None),
            P(("tile", "rep"), None),
            P(("tile", "rep")),
            P(("tile", "rep")),
            P(("tile", "rep"), None),
            P(("tile", "rep")),
            P(),
            P(),
            P(),
            P(),
            P(),
            P(),
            P(),
        ),
        out_specs=P("tile", None),
        check_vma=False,
    )
```

profile of v0, /device:TPU:2, one launch (start us, length us, event | category | flops | bytes accessed | tf_op | source)
XLA Modules:
  0.0 257.4 jit_solution(17116012527974906901)
XLA Ops:
  9.8 1.5 scatter_custom_fusion
  11.3 19.5 %all-to-all-start = ((s32[128,2,3]{2,1,0:T(2,128)}), s32[128,2,3]{2,1,0:T(2,128)S(1)}, u32[]{:S(2)}, u32[]{:S(2)}) async-start(s32[128,2,3]{2,1,0:T(2,128)} %bitcast.13), calls=%async_computation | async-start | bytes 262144 | tf_op jit(solution)/shard_map/all_to_all | solution.py:166
  31.8 4.3 %collective-permute-start = (bf16[3,64,256]{2,1,0:T(8,128)(2,1)S(1)}, bf16[3,64,256]{2,1,0:T(8,128)(2,1)S(1)}, u32[]{:S(2)}, u32[]{:S(2)}) collective-permute-start(bf16[3,64,256]{2,1,0:T(8,128)(2,1)S(1)} %slice.36), channel_id=1, source_target_pairs={{4,0},{8,4},{12,8},{16,12},{20,16},{24,20},{28,24},{32,28},{36,32}... | collective-permute-start | bytes 294920 | tf_op jit(solution)/shard_map/ppermute | solution.py:13
  37.9 1.2 fusion.74
  40.1 1.5 scatter_custom_fusion.1
  41.6 6.4 %all-to-all-done = s32[128,2,3]{2,1,0:T(2,128)S(1)} async-done(((s32[128,2,3]{2,1,0:T(2,128)}), s32[128,2,3]{2,1,0:T(2,128)S(1)}, u32[]{:S(2)}, u32[]{:S(2)}) %all-to-all-start) | async-done | bytes 3104 | tf_op jit(solution)/shard_map/all_to_all | solution.py:166
  48.0 8.2 %all-to-all-start.1 = ((bf16[128,2,32]{2,1,0:T(2,128)(2,1)}), bf16[128,2,32]{2,1,0:T(2,128)(2,1)}, u32[]{:S(2)}, u32[]{:S(2)}) async-start(bf16[128,2,32]{2,1,0:T(2,128)(2,1)} %bitcast.23), calls=%async_computation.1 | async-start | bytes 131072 | tf_op jit(solution)/shard_map/all_to_all | solution.py:165
  59.3 14.6 %gather_fusion = bf16[4096,256]{1,0:T(8,128)(2,1)S(1)} fusion(bf16[1216,256]{1,0:T(8,128)(2,1)S(1)} %bitcast.78, s32[4096]{0:T(1024)S(1)} %broadcast_clamp_fusion), kind=kCustom, calls=%fused_computation | custom fusion | bytes 4210688 | tf_op jit(solution)/shard_map/jit(_take)/gather | solution.py:83
  73.9 2.1 gather.7
  76.0 3.4 %broadcast_select_fusion = bf16[4,64,4,4,256]{4,3,2,1,0:T(4,128)(2,1)S(1)} fusion(bf16[4,64,4,4,256]{4,3,2,1,0:T(4,128)(2,1)} %gather.7, pred[4,64,4,4]{3,2,1,0:T(4,128)(4,1)S(1)} %copy.42), kind=kLoop, calls=%fused_computation.104 | loop fusion | flops 1048576 | bytes 4198400 | tf_op jit(solution)/shard_map/jit(_take)/select_n | solution.py:83
  79.4 92.5 %while.22 = (s32[]{:T(128)}, bf16[4,64,16,16]{1,3,2,0:T(8,128)(2,1)}, bf16[4,64,4,4,256]{4,3,2,1,0:T(4,128)(2,1)S(1)}, bf16[256,256]{1,0:T(8,128)(2,1)S(1)}, bf1...) while((s32[]{:T(128)}, ...), condition=%wide.region_7.8_spmd, body=%wide.region_4.7_spmd.sunk | while | flops 255102976 | bytes 30717376 | solution.py:66
  82.0 1.3 multiply_reduce_fusion.3
  83.4 10.8 %fusion.126 = bf16[4096,128]{1,0:T(8,128)(2,1)S(1)} fusion(bf16[64,128]{1,0:T(8,128)(2,1)S(1)} %copy-done.9, f32[4096,64]{1,0:T(8,128)S(1)} %reshape.309, f32[4096]{0:T(1024)S(1)} %add_rsqrt_fusion.2, f32[4096]{0:T(1024)S(1)} %broadcast_multiply_fusion.2), kind=kOutput, calls=%fused_computation.13.clone.1 | convolution fusion | flops 118751232 | bytes 2146304 | tf_op jit(solution)/shard_map/while/body/eval_jaxpr/dot_general | solution.py:46
  94.2 3.3 %reshape.310 = bf16[64,256,32]{2,1,0:T(8,128)(2,1)} reshape(bf16[4096,128]{1,0:T(8,128)(2,1)S(1)} %fusion.126) | data formatting | bytes 2097152 | tf_op jit(solution)/shard_map/while/body/eval_jaxpr/reshape | solution.py:50
  98.2 3.5 %fusion.127 = f32[64,1,256]{2,1,0:T(1,128)S(1)} fusion(bf16[64,256,32]{2,1,0:T(8,128)(2,1)} %reshape.310, bf16[64,32,1]{1,0,2:T(8,128)(2,1)S(1)} %dynamic-slice_bitcast_fusion.2), kind=kOutput, calls=%fused_computation.48.clone.1 | convolution fusion | flops 1048576 | bytes 1118208 | tf_op jit(solution)/shard_map/while/body/eval_jaxpr/nqc,nc->nq/dot_general | solution.py:52
  105.2 1.3 multiply_reduce_fusion.3
  106.5 10.8 %fusion.126 = bf16[4096,128]{1,0:T(8,128)(2,1)S(1)} fusion(bf16[64,128]{1,0:T(8,128)(2,1)S(1)} %copy-done.9, f32[4096,64]{1,0:T(8,128)S(1)} %reshape.309, f32[4096]{0:T(1024)S(1)} %add_rsqrt_fusion.2, f32[4096]{0:T(1024)S(1)} %broadcast_multiply_fusion.2), kind=kOutput, calls=%fused_computation.13.clone.1 | convolution fusion | flops 118751232 | bytes 2146304 | tf_op jit(solution)/shard_map/while/body/eval_jaxpr/dot_general | solution.py:46
  117.3 3.3 %reshape.310 = bf16[64,256,32]{2,1,0:T(8,128)(2,1)} reshape(bf16[4096,128]{1,0:T(8,128)(2,1)S(1)} %fusion.126) | data formatting | bytes 2097152 | tf_op jit(solution)/shard_map/while/body/eval_jaxpr/reshape | solution.py:50
  121.3 3.5 %fusion.127 = f32[64,1,256]{2,1,0:T(1,128)S(1)} fusion(bf16[64,256,32]{2,1,0:T(8,128)(2,1)} %reshape.310, bf16[64,32,1]{1,0,2:T(8,128)(2,1)S(1)} %dynamic-slice_bitcast_fusion.2), kind=kOutput, calls=%fused_computation.48.clone.1 | convolution fusion | flops 1048576 | bytes 1118208 | tf_op jit(solution)/shard_map/while/body/eval_jaxpr/nqc,nc->nq/dot_general | solution.py:52
  128.3 1.3 multiply_reduce_fusion.3
  129.6 10.8 %fusion.126 = bf16[4096,128]{1,0:T(8,128)(2,1)S(1)} fusion(bf16[64,128]{1,0:T(8,128)(2,1)S(1)} %copy-done.9, f32[4096,64]{1,0:T(8,128)S(1)} %reshape.309, f32[4096]{0:T(1024)S(1)} %add_rsqrt_fusion.2, f32[4096]{0:T(1024)S(1)} %broadcast_multiply_fusion.2), kind=kOutput, calls=%fused_computation.13.clone.1 | convolution fusion | flops 118751232 | bytes 2146304 | tf_op jit(solution)/shard_map/while/body/eval_jaxpr/dot_general | solution.py:46
  140.5 3.3 %reshape.310 = bf16[64,256,32]{2,1,0:T(8,128)(2,1)} reshape(bf16[4096,128]{1,0:T(8,128)(2,1)S(1)} %fusion.126) | data formatting | bytes 2097152 | tf_op jit(solution)/shard_map/while/body/eval_jaxpr/reshape | solution.py:50
  144.5 3.5 %fusion.127 = f32[64,1,256]{2,1,0:T(1,128)S(1)} fusion(bf16[64,256,32]{2,1,0:T(8,128)(2,1)} %reshape.310, bf16[64,32,1]{1,0,2:T(8,128)(2,1)S(1)} %dynamic-slice_bitcast_fusion.2), kind=kOutput, calls=%fused_computation.48.clone.1 | convolution fusion | flops 1048576 | bytes 1118208 | tf_op jit(solution)/shard_map/while/body/eval_jaxpr/nqc,nc->nq/dot_general | solution.py:52
  151.4 1.3 multiply_reduce_fusion.3
  152.7 10.8 %fusion.126 = bf16[4096,128]{1,0:T(8,128)(2,1)S(1)} fusion(bf16[64,128]{1,0:T(8,128)(2,1)S(1)} %copy-done.9, f32[4096,64]{1,0:T(8,128)S(1)} %reshape.309, f32[4096]{0:T(1024)S(1)} %add_rsqrt_fusion.2, f32[4096]{0:T(1024)S(1)} %broadcast_multiply_fusion.2), kind=kOutput, calls=%fused_computation.13.clone.1 | convolution fusion | flops 118751232 | bytes 2146304 | tf_op jit(solution)/shard_map/while/body/eval_jaxpr/dot_general | solution.py:46
  163.6 3.3 %reshape.310 = bf16[64,256,32]{2,1,0:T(8,128)(2,1)} reshape(bf16[4096,128]{1,0:T(8,128)(2,1)S(1)} %fusion.126) | data formatting | bytes 2097152 | tf_op jit(solution)/shard_map/while/body/eval_jaxpr/reshape | solution.py:50
  167.6 3.5 %fusion.127 = f32[64,1,256]{2,1,0:T(1,128)S(1)} fusion(bf16[64,256,32]{2,1,0:T(8,128)(2,1)} %reshape.310, bf16[64,32,1]{1,0,2:T(8,128)(2,1)S(1)} %dynamic-slice_bitcast_fusion.2), kind=kOutput, calls=%fused_computation.48.clone.1 | convolution fusion | flops 1048576 | bytes 1118208 | tf_op jit(solution)/shard_map/while/body/eval_jaxpr/nqc,nc->nq/dot_general | solution.py:52
  172.0 11.3 %while.23 = (s32[]{:T(128)}, f32[76,256]{1,0:T(8,128)S(1)}, s32[4,64]{1,0:T(4,128)}, bf16[4,64,16,16]{1,3,2,0:T(8,128)(2,1)}, s32[4,64]{1,0:T(4,128)}, /*index=5*/s32[]{:T(128)}, s32[]{:T(128)}) while((s32[]{:T(128)}, f32[76,256]{1,0:T(8,128)S(1)}, s32[4,64]{1,0:T(4,128)}, bf16[4,64,16,16]{1,3,2,0:T(8,128)(2,1)}, ...), condition=%wide.region_9.10_spmd.clone.clone, body=%wide.region_8.9_spmd.clone.clone.sunk | while | flops 48877696 | bytes 1394271 | solution.py:114
  183.9 57.3 %all-reduce.3.cloned.1.call-done = f32[76,256]{1,0:T(8,128)} async-done(((f32[76,256]{1,0:T(8,128)}), f32[76,256]{1,0:T(8,128)}) %all-reduce.3.cloned.1.call-update) | async-done | bytes 77840 | tf_op jit(solution)/shard_map/psum | solution.py:187
  241.9 1.9 collective-permute-start.1
  243.8 5.2 %collective-permute-done.1 = f32[12,256]{1,0:T(8,128)S(1)} collective-permute-done((f32[12,256]{1,0:T(8,128)S(1)}, f32[12,256]{1,0:T(8,128)S(1)}, u32[]{:S(2)}, u32[]{:S(2)}) %collective-permute-start.1) | collective-permute-done | bytes 12320 | tf_op jit(solution)/shard_map/ppermute | solution.py:13
  249.0 1.5 slice_add_fusion
  (155 shorter events, 38.9 us)
Async XLA Ops:
  6.5 31.3 %copy-start = (bf16[256,256]{1,0:T(8,128)(2,1)S(1)}, bf16[256,256]{1,0:T(8,128)(2,1)}, u32[]{:S(2)}) copy-start(bf16[256,256]{1,0:T(8,128)(2,1)} %param.26) | copy-start | bytes 393220
  11.3 36.7 %all-to-all-start = ((s32[128,2,3]{2,1,0:T(2,128)}), s32[128,2,3]{2,1,0:T(2,128)S(1)}, u32[]{:S(2)}, u32[]{:S(2)}) async-start(s32[128,2,3]{2,1,0:T(2,128)} %bitcast.13), calls=%async_computation | async-start | bytes 262144 | tf_op jit(solution)/shard_map/all_to_all | solution.py:166
  30.8 28.4 %copy-start.4 = (bf16[16,64,256]{2,1,0:T(8,128)(2,1)S(1)}, bf16[16,64,256]{2,1,0:T(8,128)(2,1)}, u32[]{:S(2)}) copy-start(bf16[16,64,256]{2,1,0:T(8,128)(2,1)} %param.17) | copy-start | bytes 1572868
  31.8 27.4 %collective-permute-start = (bf16[3,64,256]{2,1,0:T(8,128)(2,1)S(1)}, bf16[3,64,256]{2,1,0:T(8,128)(2,1)S(1)}, u32[]{:S(2)}, u32[]{:S(2)}) collective-permute-start(bf16[3,64,256]{2,1,0:T(8,128)(2,1)S(1)} %slice.36), channel_id=1, source_target_pairs={{4,0},{8,4},{12,8},{16,12},{20,16},{24,20},{28,24},{32,28},{36,32}... | collective-permute-start | bytes 294920 | tf_op jit(solution)/shard_map/ppermute | solution.py:13
  48.0 31.4 %all-to-all-start.1 = ((bf16[128,2,32]{2,1,0:T(2,128)(2,1)}), bf16[128,2,32]{2,1,0:T(2,128)(2,1)}, u32[]{:S(2)}, u32[]{:S(2)}) async-start(bf16[128,2,32]{2,1,0:T(2,128)(2,1)} %bitcast.23), calls=%async_computation.1 | async-start | bytes 131072 | tf_op jit(solution)/shard_map/all_to_all | solution.py:165
  56.2 185.0 %all-reduce.3.cloned.1.call-start = ((), (), s32[]{:S(2)}) async-start(), calls=%async_computation.2 | async-start | bytes 163840 | tf_op jit(solution)/shard_map/psum | solution.py:187
  56.7 0.6 copy-start.7
  56.8 0.6 copy-start.8
  76.0 3.4 %copy-start.3 = (bf16[256,256]{1,0:T(8,128)(2,1)S(1)}, bf16[256,256]{1,0:T(8,128)(2,1)}, u32[]{:S(2)}) copy-start(bf16[256,256]{1,0:T(8,128)(2,1)} %param.28) | copy-start | bytes 393220
  79.4 92.5 %copy-start.5 = (f32[76,256]{1,0:T(8,128)S(1)}, f32[76,256]{1,0:T(8,128)}, u32[]{:S(2)}) copy-start(f32[76,256]{1,0:T(8,128)} %custom-call) | copy-start | bytes 233476
  79.4 1.3 copy-start.1
  81.4 1.9 copy-start.9
  98.2 4.3 %copy-start.2 = (bf16[4,64,4,4,256]{4,3,2,1,0:T(4,128)(2,1)S(1)}, bf16[4,64,4,4,256]{4,3,2,1,0:T(4,128)(2,1)}, u32[]{:S(2)}) copy-start(bf16[4,64,4,4,256]{4,3,2,1,0:T(4,128)(2,1)} %copy-done.1) | copy-start | bytes 6291460 | tf_op jit(solution)/shard_map/while
  102.6 1.3 copy-start.1
  104.5 1.9 copy-start.9
  121.3 4.4 %copy-start.2 = (bf16[4,64,4,4,256]{4,3,2,1,0:T(4,128)(2,1)S(1)}, bf16[4,64,4,4,256]{4,3,2,1,0:T(4,128)(2,1)}, u32[]{:S(2)}) copy-start(bf16[4,64,4,4,256]{4,3,2,1,0:T(4,128)(2,1)} %copy-done.1) | copy-start | bytes 6291460 | tf_op jit(solution)/shard_map/while
  125.7 1.3 copy-start.1
  127.7 1.9 copy-start.9
  144.5 4.4 %copy-start.2 = (bf16[4,64,4,4,256]{4,3,2,1,0:T(4,128)(2,1)S(1)}, bf16[4,64,4,4,256]{4,3,2,1,0:T(4,128)(2,1)}, u32[]{:S(2)}) copy-start(bf16[4,64,4,4,256]{4,3,2,1,0:T(4,128)(2,1)} %copy-done.1) | copy-start | bytes 6291460 | tf_op jit(solution)/shard_map/while
  148.8 1.3 copy-start.1
  150.8 1.9 copy-start.9
  167.6 4.4 %copy-start.2 = (bf16[4,64,4,4,256]{4,3,2,1,0:T(4,128)(2,1)S(1)}, bf16[4,64,4,4,256]{4,3,2,1,0:T(4,128)(2,1)}, u32[]{:S(2)}) copy-start(bf16[4,64,4,4,256]{4,3,2,1,0:T(4,128)(2,1)} %copy-done.1) | copy-start | bytes 6291460 | tf_op jit(solution)/shard_map/while
  183.2 0.6 copy-start.6
  241.9 7.2 %collective-permute-start.1 = (f32[12,256]{1,0:T(8,128)S(1)}, f32[12,256]{1,0:T(8,128)S(1)}, u32[]{:S(2)}, u32[]{:S(2)}) collective-permute-start(f32[12,256]{1,0:T(8,128)S(1)} %slice.51), channel_id=1, source_target_pairs={{0,4},{4,8},{8,12},{12,16},{16,20},{20,24},{24,28},{28,32},{32,36}... | collective-permute-start | bytes 36872 | tf_op jit(solution)/shard_map/ppermute | solution.py:13
Sparse Core Ops, SparseCore 0:
  184.0 57.0 all-reduce.2
where the time goes:
time: 258 us; the launch traced here: 257 us
  waiting for transfers between devices  69 us (27%)
  matrix products  64.2 us (25%)
  local copies, waits for them, and re-layouts  53.2 us (21%)
  starting transfers between devices  34.1 us (13%)
  other arithmetic  22.7 us (9%)
  between operations  13.6 us (5%)
    psum x1, waiting for transfers between devices, on_device(): summed = lax.psum(canvas, 'rep')  57.3 us
    dot_general x4, matrix products, mask_terms(): second = jnp.dot(active, conv_two, preferred_element_type=jnp.float32)  43.4 us
    all_to_all x1, starting transfers between devices, on_device(): lax.all_to_all(request_slots, 'tile', split_axis=0, concat_axis=0, tiled=...  19.5 us
    gather x2, local copies, waits for them, and re-layouts, cut_crops(): jnp.take(extended.reshape(height * width, channels), cell_index, axis=0)  16.7 us
    dot_general x4, matrix products, mask_terms(): jnp.einsum('nqc,nc->nq', upscaled, head_rows, preferred_element_type=jnp....  14 us
    reshape x4, local copies, waits for them, and re-layouts, mask_terms(): upscaled = jax.nn.gelu(second, approximate=False).astype(jnp.bfloat16).re...  13.1 us
    all_to_all x1, starting transfers between devices, on_device(): lax.all_to_all(head_slots, 'tile', split_axis=0, concat_axis=0, tiled=True)  8.16 us
    all_to_all x1, waiting for transfers between devices, on_device(): lax.all_to_all(request_slots, 'tile', split_axis=0, concat_axis=0, tiled=...  6.42 us
  transfers between devices with their start and end apart: 5, of which 3 were waited for; matrix products, arithmetic and copies ran while one was open for 11% of the time, Pallas kernels for 0%

commit v1 on v0

--- a/solution.py
+++ b/solution.py
@@ -184,7 +184,11 @@
         4 * strip_height + 4 * CK - 4,
         breadth,
     )
-    summed = lax.psum(canvas, "rep")
+
+    def list_meshes(axis_key, local_x):
+        return jax.lax.all_gather(local_x, axis_name=axis_key).sum(axis=0)
+
+    summed = list_meshes("rep", canvas)
     spilled = shifted(summed[4 * strip_height :], "tile", 1)
     return summed[: 4 * strip_height] + jnp.pad(
         spilled, ((0, 4 * strip_height - spilled.shape[0]), (0, 0))

time: 258 us -> 199 us (0.77)
  the two profiles are of different devices: /device:TPU:2 before, /device:TPU:6 now
where the time goes in v1:
time: 199 us; the launch traced here: 198 us
  matrix products  64.2 us (32%)
  local copies, waits for them, and re-layouts  51.9 us (26%)
  starting transfers between devices  35.8 us (18%)
  other arithmetic  21.8 us (11%)
  blocking collectives  12.9 us (6%)
  waiting for transfers between devices  10.2 us (5%)
    dot_general x4, matrix products, mask_terms(): second = jnp.dot(active, conv_two, preferred_element_type=jnp.float32)  43.4 us
    all_to_all x1, starting transfers between devices, on_device(): lax.all_to_all(request_slots, 'tile', split_axis=0, concat_axis=0, tiled=...  19.9 us
    gather x2, local copies, waits for them, and re-layouts, cut_crops(): jnp.take(extended.reshape(height * width, channels), cell_index, axis=0)  16.7 us
    dot_general x4, matrix products, mask_terms(): jnp.einsum('nqc,nc->nq', upscaled, head_rows, preferred_element_type=jnp....  14 us
    reshape x4, local copies, waits for them, and re-layouts, mask_terms(): upscaled = jax.nn.gelu(second, approximate=False).astype(jnp.bfloat16).re...  13.1 us
    all_gather x1, blocking collectives, list_meshes(): return jax.lax.all_gather(local_x, axis_name=axis_key).sum(axis=0)  12.9 us
    all_to_all x1, starting transfers between devices, on_device(): lax.all_to_all(head_slots, 'tile', split_axis=0, concat_axis=0, tiled=True)  9.39 us
    ppermute x2, starting transfers between devices, shifted(): lax.ppermute(value, axis, [(source, source + steps) for source in range(l...  6.5 us
  transfers between devices with their start and end apart: 4, of which 2 were waited for; matrix products, arithmetic and copies ran while one was open for 15% of the time, Pallas kernels for 0%

profile of v1, /device:TPU:6, one launch (start us, length us, event | category | flops | bytes accessed | tf_op | source)
XLA Modules:
  0.0 197.6 jit_solution(7991645341286870856)
XLA Ops:
  3.3 1.5 scatter_custom_fusion
  4.7 19.9 %all-to-all-start = ((s32[128,2,3]{2,1,0:T(2,128)}), s32[128,2,3]{2,1,0:T(2,128)S(1)}, u32[]{:S(2)}, u32[]{:S(2)}) async-start(s32[128,2,3]{2,1,0:T(2,128)} %bitcast.13), calls=%async_computation | async-start | bytes 262144 | tf_op jit(solution)/shard_map/all_to_all | solution.py:166
  25.6 4.6 %collective-permute-start = (bf16[3,64,256]{2,1,0:T(8,128)(2,1)S(1)}, bf16[3,64,256]{2,1,0:T(8,128)(2,1)S(1)}, u32[]{:S(2)}, u32[]{:S(2)}) collective-permute-start(bf16[3,64,256]{2,1,0:T(8,128)(2,1)S(1)} %slice.36), channel_id=1, source_target_pairs={{4,0},{8,4},{12,8},{16,12},{20,16},{24,20},{28,24},{32,28},{36,32}... | collective-permute-start | bytes 294920 | tf_op jit(solution)/shard_map/ppermute | solution.py:13
  32.0 1.2 fusion.74
  34.2 1.5 scatter_custom_fusion.1
  35.7 5.0 %all-to-all-done = s32[128,2,3]{2,1,0:T(2,128)S(1)} async-done(((s32[128,2,3]{2,1,0:T(2,128)}), s32[128,2,3]{2,1,0:T(2,128)S(1)}, u32[]{:S(2)}, u32[]{:S(2)}) %all-to-all-start) | async-done | bytes 3104 | tf_op jit(solution)/shard_map/all_to_all | solution.py:166
  40.6 9.4 %all-to-all-start.1 = ((bf16[128,2,32]{2,1,0:T(2,128)(2,1)}), bf16[128,2,32]{2,1,0:T(2,128)(2,1)}, u32[]{:S(2)}, u32[]{:S(2)}) async-start(bf16[128,2,32]{2,1,0:T(2,128)(2,1)} %bitcast.23), calls=%async_computation.1 | async-start | bytes 131072 | tf_op jit(solution)/shard_map/all_to_all | solution.py:165
  52.9 14.6 %gather_fusion = bf16[4096,256]{1,0:T(8,128)(2,1)S(1)} fusion(bf16[1216,256]{1,0:T(8,128)(2,1)S(1)} %bitcast.79, s32[4096]{0:T(1024)S(1)} %broadcast_clamp_fusion), kind=kCustom, calls=%fused_computation | custom fusion | bytes 4210688 | tf_op jit(solution)/shard_map/jit(_take)/gather | solution.py:83
  67.5 2.1 %gather.7 = bf16[4,64,4,4,256]{4,3,2,1,0:T(4,128)(2,1)} reshape(bf16[4096,256]{1,0:T(8,128)(2,1)S(1)} %gather_fusion) | data formatting | bytes 4194304 | tf_op jit(solution)/shard_map/jit(_take)/gather | solution.py:83
  69.6 3.4 %broadcast_select_fusion = bf16[4,64,4,4,256]{4,3,2,1,0:T(4,128)(2,1)S(1)} fusion(bf16[4,64,4,4,256]{4,3,2,1,0:T(4,128)(2,1)} %gather.7, pred[4,64,4,4]{3,2,1,0:T(4,128)(4,1)S(1)} %copy.42), kind=kLoop, calls=%fused_computation.104 | loop fusion | flops 1048576 | bytes 4198400 | tf_op jit(solution)/shard_map/jit(_take)/select_n | solution.py:83
  73.1 92.5 %while.22 = (s32[]{:T(128)}, bf16[4,64,16,16]{1,3,2,0:T(8,128)(2,1)}, bf16[4,64,4,4,256]{4,3,2,1,0:T(4,128)(2,1)S(1)}, bf16[256,256]{1,0:T(8,128)(2,1)S(1)}, bf1...) while((s32[]{:T(128)}, ...), condition=%wide.region_7.8_spmd, body=%wide.region_4.7_spmd.sunk | while | flops 255102976 | bytes 30717376 | solution.py:66
  75.7 1.3 multiply_reduce_fusion.3
  77.0 10.8 %fusion.126 = bf16[4096,128]{1,0:T(8,128)(2,1)S(1)} fusion(bf16[64,128]{1,0:T(8,128)(2,1)S(1)} %copy-done.8, f32[4096,64]{1,0:T(8,128)S(1)} %reshape.313, f32[4096]{0:T(1024)S(1)} %add_rsqrt_fusion.2, f32[4096]{0:T(1024)S(1)} %broadcast_multiply_fusion.2), kind=kOutput, calls=%fused_computation.13.clone.1 | convolution fusion | flops 118751232 | bytes 2146304 | tf_op jit(solution)/shard_map/while/body/eval_jaxpr/dot_general | solution.py:46
  87.9 3.3 %reshape.314 = bf16[64,256,32]{2,1,0:T(8,128)(2,1)} reshape(bf16[4096,128]{1,0:T(8,128)(2,1)S(1)} %fusion.126) | data formatting | bytes 2097152 | tf_op jit(solution)/shard_map/while/body/eval_jaxpr/reshape | solution.py:50
  91.9 3.5 %fusion.127 = f32[64,1,256]{2,1,0:T(1,128)S(1)} fusion(bf16[64,256,32]{2,1,0:T(8,128)(2,1)} %reshape.314, bf16[64,32,1]{1,0,2:T(8,128)(2,1)S(1)} %dynamic-slice_bitcast_fusion.2), kind=kOutput, calls=%fused_computation.48.clone.1 | convolution fusion | flops 1048576 | bytes 1118208 | tf_op jit(solution)/shard_map/while/body/eval_jaxpr/nqc,nc->nq/dot_general | solution.py:52
  96.5 1.0 copy-done.1
  98.8 1.3 multiply_reduce_fusion.3
  100.1 10.8 %fusion.126 = bf16[4096,128]{1,0:T(8,128)(2,1)S(1)} fusion(bf16[64,128]{1,0:T(8,128)(2,1)S(1)} %copy-done.8, f32[4096,64]{1,0:T(8,128)S(1)} %reshape.313, f32[4096]{0:T(1024)S(1)} %add_rsqrt_fusion.2, f32[4096]{0:T(1024)S(1)} %broadcast_multiply_fusion.2), kind=kOutput, calls=%fused_computation.13.clone.1 | convolution fusion | flops 118751232 | bytes 2146304 | tf_op jit(solution)/shard_map/while/body/eval_jaxpr/dot_general | solution.py:46
  111.0 3.3 %reshape.314 = bf16[64,256,32]{2,1,0:T(8,128)(2,1)} reshape(bf16[4096,128]{1,0:T(8,128)(2,1)S(1)} %fusion.126) | data formatting | bytes 2097152 | tf_op jit(solution)/shard_map/while/body/eval_jaxpr/reshape | solution.py:50
  115.0 3.5 %fusion.127 = f32[64,1,256]{2,1,0:T(1,128)S(1)} fusion(bf16[64,256,32]{2,1,0:T(8,128)(2,1)} %reshape.314, bf16[64,32,1]{1,0,2:T(8,128)(2,1)S(1)} %dynamic-slice_bitcast_fusion.2), kind=kOutput, calls=%fused_computation.48.clone.1 | convolution fusion | flops 1048576 | bytes 1118208 | tf_op jit(solution)/shard_map/while/body/eval_jaxpr/nqc,nc->nq/dot_general | solution.py:52
  121.9 1.3 multiply_reduce_fusion.3
  123.3 10.8 %fusion.126 = bf16[4096,128]{1,0:T(8,128)(2,1)S(1)} fusion(bf16[64,128]{1,0:T(8,128)(2,1)S(1)} %copy-done.8, f32[4096,64]{1,0:T(8,128)S(1)} %reshape.313, f32[4096]{0:T(1024)S(1)} %add_rsqrt_fusion.2, f32[4096]{0:T(1024)S(1)} %broadcast_multiply_fusion.2), kind=kOutput, calls=%fused_computation.13.clone.1 | convolution fusion | flops 118751232 | bytes 2146304 | tf_op jit(solution)/shard_map/while/body/eval_jaxpr/dot_general | solution.py:46
  134.1 3.3 %reshape.314 = bf16[64,256,32]{2,1,0:T(8,128)(2,1)} reshape(bf16[4096,128]{1,0:T(8,128)(2,1)S(1)} %fusion.126) | data formatting | bytes 2097152 | tf_op jit(solution)/shard_map/while/body/eval_jaxpr/reshape | solution.py:50
  138.1 3.5 %fusion.127 = f32[64,1,256]{2,1,0:T(1,128)S(1)} fusion(bf16[64,256,32]{2,1,0:T(8,128)(2,1)} %reshape.314, bf16[64,32,1]{1,0,2:T(8,128)(2,1)S(1)} %dynamic-slice_bitcast_fusion.2), kind=kOutput, calls=%fused_computation.48.clone.1 | convolution fusion | flops 1048576 | bytes 1118208 | tf_op jit(solution)/shard_map/while/body/eval_jaxpr/nqc,nc->nq/dot_general | solution.py:52
  145.1 1.3 multiply_reduce_fusion.3
  146.4 10.8 %fusion.126 = bf16[4096,128]{1,0:T(8,128)(2,1)S(1)} fusion(bf16[64,128]{1,0:T(8,128)(2,1)S(1)} %copy-done.8, f32[4096,64]{1,0:T(8,128)S(1)} %reshape.313, f32[4096]{0:T(1024)S(1)} %add_rsqrt_fusion.2, f32[4096]{0:T(1024)S(1)} %broadcast_multiply_fusion.2), kind=kOutput, calls=%fused_computation.13.clone.1 | convolution fusion | flops 118751232 | bytes 2146304 | tf_op jit(solution)/shard_map/while/body/eval_jaxpr/dot_general | solution.py:46
  157.2 3.3 %reshape.314 = bf16[64,256,32]{2,1,0:T(8,128)(2,1)} reshape(bf16[4096,128]{1,0:T(8,128)(2,1)S(1)} %fusion.126) | data formatting | bytes 2097152 | tf_op jit(solution)/shard_map/while/body/eval_jaxpr/reshape | solution.py:50
  161.2 3.5 %fusion.127 = f32[64,1,256]{2,1,0:T(1,128)S(1)} fusion(bf16[64,256,32]{2,1,0:T(8,128)(2,1)} %reshape.314, bf16[64,32,1]{1,0,2:T(8,128)(2,1)S(1)} %dynamic-slice_bitcast_fusion.2), kind=kOutput, calls=%fused_computation.48.clone.1 | convolution fusion | flops 1048576 | bytes 1118208 | tf_op jit(solution)/shard_map/while/body/eval_jaxpr/nqc,nc->nq/dot_general | solution.py:52
  165.6 11.3 %while.23 = (s32[]{:T(128)}, f32[76,256]{1,0:T(8,128)S(1)}, s32[4,64]{1,0:T(4,128)}, bf16[4,64,16,16]{1,3,2,0:T(8,128)(2,1)}, s32[4,64]{1,0:T(4,128)}, /*index=5*/s32[]{:T(128)}, s32[]{:T(128)}) while((s32[]{:T(128)}, f32[76,256]{1,0:T(8,128)S(1)}, s32[4,64]{1,0:T(4,128)}, bf16[4,64,16,16]{1,3,2,0:T(8,128)(2,1)}, ...), condition=%wide.region_9.10_spmd.clone.clone, body=%wide.region_8.9_spmd.clone.clone.sunk | while | flops 48877696 | bytes 1394271 | solution.py:114
  176.9 12.9 %all-gather.1 = f32[4,76,256]{2,1,0:T(8,128)S(1)} all-gather(f32[1,76,256]{2,1,0:T(8,128)S(1)} %bitcast.83), channel_id=2, replica_groups=mesh['tile'=128,'rep'=4] {'rep'}, dimensions={0}, use_global_device_ids=true | all-gather | bytes 389120 | tf_op jit(solution)/shard_map/all_gather | solution.py:189
  189.8 1.9 collective-permute-start.1
  191.7 5.2 %collective-permute-done.1 = f32[12,256]{1,0:T(8,128)S(1)} collective-permute-done((f32[12,256]{1,0:T(8,128)S(1)}, f32[12,256]{1,0:T(8,128)S(1)}, u32[]{:S(2)}, u32[]{:S(2)}) %collective-permute-start.1) | collective-permute-done | bytes 12320 | tf_op jit(solution)/shard_map/ppermute | solution.py:13
  (152 shorter events, 37.0 us)
Async XLA Ops:
  0.0 32.0 %copy-start = (bf16[256,256]{1,0:T(8,128)(2,1)S(1)}, bf16[256,256]{1,0:T(8,128)(2,1)}, u32[]{:S(2)}) copy-start(bf16[256,256]{1,0:T(8,128)(2,1)} %param.26) | copy-start | bytes 393220
  4.7 35.9 %all-to-all-start = ((s32[128,2,3]{2,1,0:T(2,128)}), s32[128,2,3]{2,1,0:T(2,128)S(1)}, u32[]{:S(2)}, u32[]{:S(2)}) async-start(s32[128,2,3]{2,1,0:T(2,128)} %bitcast.13), calls=%async_computation | async-start | bytes 262144 | tf_op jit(solution)/shard_map/all_to_all | solution.py:166
  24.6 28.2 %copy-start.4 = (bf16[16,64,256]{2,1,0:T(8,128)(2,1)S(1)}, bf16[16,64,256]{2,1,0:T(8,128)(2,1)}, u32[]{:S(2)}) copy-start(bf16[16,64,256]{2,1,0:T(8,128)(2,1)} %param.17) | copy-start | bytes 1572868
  25.6 27.2 %collective-permute-start = (bf16[3,64,256]{2,1,0:T(8,128)(2,1)S(1)}, bf16[3,64,256]{2,1,0:T(8,128)(2,1)S(1)}, u32[]{:S(2)}, u32[]{:S(2)}) collective-permute-start(bf16[3,64,256]{2,1,0:T(8,128)(2,1)S(1)} %slice.36), channel_id=1, source_target_pairs={{4,0},{8,4},{12,8},{16,12},{20,16},{24,20},{28,24},{32,28},{36,32}... | collective-permute-start | bytes 294920 | tf_op jit(solution)/shard_map/ppermute | solution.py:13
  40.6 32.4 %all-to-all-start.1 = ((bf16[128,2,32]{2,1,0:T(2,128)(2,1)}), bf16[128,2,32]{2,1,0:T(2,128)(2,1)}, u32[]{:S(2)}, u32[]{:S(2)}) async-start(bf16[128,2,32]{2,1,0:T(2,128)(2,1)} %bitcast.23), calls=%async_computation.1 | async-start | bytes 131072 | tf_op jit(solution)/shard_map/all_to_all | solution.py:165
  50.4 0.6 copy-start.6
  50.5 0.6 copy-start.7
  69.6 3.4 %copy-start.3 = (bf16[256,256]{1,0:T(8,128)(2,1)S(1)}, bf16[256,256]{1,0:T(8,128)(2,1)}, u32[]{:S(2)}) copy-start(bf16[256,256]{1,0:T(8,128)(2,1)} %param.28) | copy-start | bytes 393220
  73.1 92.5 %copy-start.5 = (f32[76,256]{1,0:T(8,128)S(1)}, f32[76,256]{1,0:T(8,128)}, u32[]{:S(2)}) copy-start(f32[76,256]{1,0:T(8,128)} %custom-call) | copy-start | bytes 233476
  73.1 1.3 copy-start.1
  75.1 1.9 copy-start.8
  91.9 4.3 %copy-start.2 = (bf16[4,64,4,4,256]{4,3,2,1,0:T(4,128)(2,1)S(1)}, bf16[4,64,4,4,256]{4,3,2,1,0:T(4,128)(2,1)}, u32[]{:S(2)}) copy-start(bf16[4,64,4,4,256]{4,3,2,1,0:T(4,128)(2,1)} %copy-done.1) | copy-start | bytes 6291460 | tf_op jit(solution)/shard_map/while
  96.2 1.3 copy-start.1
  98.2 1.9 copy-start.8
  115.0 4.3 %copy-start.2 = (bf16[4,64,4,4,256]{4,3,2,1,0:T(4,128)(2,1)S(1)}, bf16[4,64,4,4,256]{4,3,2,1,0:T(4,128)(2,1)}, u32[]{:S(2)}) copy-start(bf16[4,64,4,4,256]{4,3,2,1,0:T(4,128)(2,1)} %copy-done.1) | copy-start | bytes 6291460 | tf_op jit(solution)/shard_map/while
  119.3 1.3 copy-start.1
  121.3 1.9 copy-start.8
  138.1 4.3 %copy-start.2 = (bf16[4,64,4,4,256]{4,3,2,1,0:T(4,128)(2,1)S(1)}, bf16[4,64,4,4,256]{4,3,2,1,0:T(4,128)(2,1)}, u32[]{:S(2)}) copy-start(bf16[4,64,4,4,256]{4,3,2,1,0:T(4,128)(2,1)} %copy-done.1) | copy-start | bytes 6291460 | tf_op jit(solution)/shard_map/while
  142.5 1.3 copy-start.1
  144.4 1.9 copy-start.8
  161.2 4.3 %copy-start.2 = (bf16[4,64,4,4,256]{4,3,2,1,0:T(4,128)(2,1)S(1)}, bf16[4,64,4,4,256]{4,3,2,1,0:T(4,128)(2,1)}, u32[]{:S(2)}) copy-start(bf16[4,64,4,4,256]{4,3,2,1,0:T(4,128)(2,1)} %copy-done.1) | copy-start | bytes 6291460 | tf_op jit(solution)/shard_map/while
  189.8 7.2 %collective-permute-start.1 = (f32[12,256]{1,0:T(8,128)S(1)}, f32[12,256]{1,0:T(8,128)S(1)}, u32[]{:S(2)}, u32[]{:S(2)}) collective-permute-start(f32[12,256]{1,0:T(8,128)S(1)} %slice.51), channel_id=1, source_target_pairs={{0,4},{4,8},{8,12},{12,16},{16,20},{20,24},{24,28},{28,32},{32,36}... | collective-permute-start | bytes 36872 | tf_op jit(solution)/shard_map/ppermute | solution.py:13
